TPU v7x, 128 devices: a whole 4x4x4 slice. The times are simulated.
128 devices in a mesh: tm: 32 (over z, y, core), row: 4 (over x).
Axes of the slice: x: 4, y: 4, z: 4, core: 2. Of those that a mesh axis runs over, the one named last changes fastest.
Arguments:
- edge_factor: float32 [32, 512, 512], P('tm', 'row'), may hold values from -0.25 to 0.25
- mass: float32 [32, 512], P('tm', 'row'), may hold values from 0.001 to 0.01
- rhs: float32 [32, 512, 512], P('tm', None, 'row'), may hold values from -0.25 to 0.25
Outputs:
- solution: float32 [32, 512, 512], P('tm', None, 'row')
All inputs are finite; a program needn't handle non-finite values.
Results may differ from a plain program's by a relative error of at most 0.0003.
Values sent between devices are 32-bit elements; how exact they have to be, the bound alone decides.
A program may use at most 128 MiB of HBM per device.

v0:
```python
import jax
import jax.numpy as jnp
from jax import lax
from jax.sharding import PartitionSpec as P

exact_prec = lax.Precision.HIGHEST


def passed_along(block, axis, distance):
    devices = range(lax.axis_size(axis))
    route = [(i - distance, i) for i in devices if i - distance in devices]
    return lax.ppermute(block, axis, route)


def solve_lower(factor, values):
    return jax.scipy.linalg.solve_triangular(factor, values, lower=True)


def block_cholesky(matrix):
    half = matrix.shape[0] // 2
    upper_left = jnp.linalg.cholesky(matrix[:half, :half])
    lower_left = solve_lower(upper_left, matrix[:half, half:]).T
    schur_part = matrix[half:, half:] - jnp.dot(lower_left, lower_left.T, precision=exact_prec)
    lower_right = jnp.linalg.cholesky(schur_part)
    top_rows = jnp.concatenate(
        [upper_left, jnp.zeros((half, matrix.shape[0] - half), jnp.float32)], axis=1
    )
    bottom_rows = jnp.concatenate([lower_left, lower_right], axis=1)
    return jnp.concatenate([top_rows, bottom_rows], axis=0)


def factor_split(diag_part):
    full_diag = lax.all_gather(diag_part, "row", axis=1, tiled=True)
    return block_cholesky(full_diag)


def local(edge_factor, mass, rhs):
    factor_rows = edge_factor[0]
    mass_rows = mass[0]
    rhs_cols = rhs[0]
    quarter = factor_rows.shape[0]
    node_count = factor_rows.shape[1]
    blocks = lax.axis_size("tm")
    at_start = lax.axis_index("tm") == 0
    edge_cols = jnp.dot(
        lax.all_gather(factor_rows, "row", axis=0, tiled=True),
        factor_rows.T,
        precision=exact_prec,
        preferred_element_type=jnp.float32,
    )
    edge_next = passed_along(edge_cols, "tm", -1)
    offset = lax.axis_index("row") * quarter
    row_ids = lax.broadcasted_iota(jnp.int32, (node_count, quarter), 0)
    col_ids = lax.broadcasted_iota(jnp.int32, (node_count, quarter), 1) + offset
    mass_diag = jnp.where(row_ids == col_ids, mass_rows[None, :], 0.0)
    diag_part = mass_diag + edge_cols + edge_next
    low_coupling = jnp.where(at_start, 0.0, -edge_cols)
    up_coupling = -edge_next
    stride = 1
    while stride < blocks:
        factor = factor_split(diag_part)
        whitened = solve_lower(
            factor, jnp.concatenate([low_coupling, up_coupling, rhs_cols], axis=1)
        )
        stacked = jnp.stack([whitened[:, :quarter], whitened[:, quarter : 2 * quarter]])
        gram_blocks = jnp.einsum(
            "tbn,bk->tnk",
            lax.all_gather(stacked, "row", axis=2, tiled=True),
            whitened,
            precision=exact_prec,
        )
        from_below = passed_along(gram_blocks[1], "tm", stride)
        from_above = passed_along(gram_blocks[0], "tm", -stride)
        diag_part = diag_part - from_below[:, quarter : 2 * quarter] - from_above[:, :quarter]
        low_coupling = -from_below[:, :quarter]
        up_coupling = -from_above[:, quarter : 2 * quarter]
        rhs_cols = rhs_cols - from_below[:, 2 * quarter :] - from_above[:, 2 * quarter :]
        stride = stride * 2
    factor = factor_split(diag_part)
    inner = solve_lower(factor, rhs_cols)
    solution = jax.scipy.linalg.solve_triangular(factor, inner, lower=True, trans=1)
    return solution[None]


def solution(mesh):
    placed = (P("tm", "row", None), P("tm", "row"), P("tm", None, "row"))
    return jax.shard_map(
        local, mesh=mesh, in_specs=placed, out_specs=P("tm", None, "row"), check_vma=False
    )
```

profile of v0, /device:TPU:16, one launch (start us, length us, event | category | flops | bytes accessed | tf_op | source)
XLA Modules:
  0.0 1456.2 jit_solution(16818976105928106084)
XLA Ops:
  7.3 28.0 %all-gather.36.cloned.1.call-done = f32[1,512,512]{2,1,0:T(8,128)} async-done(((f32[1,128,512]{2,1,0:T(8,128)}), f32[1,512,512]{2,1,0:T(8,128)}) %all-gather.36.cloned.1.call-update) | async-done | bytes 1048592 | tf_op jit(solution)/shard_map/all_gather | solution.py:46
  45.3 26.0 %all-gather.14.cloned.1.call-done = f32[512,512]{0,1:T(8,128)} async-done(((f32[512,128]{0,1:T(8,128)}), f32[512,512]{0,1:T(8,128)}) %all-gather.14.cloned.1.call-update) | async-done | bytes 1048592 | tf_op jit(solution)/shard_map/all_gather | solution.py:33
  113.7 19.7 %custom-call.43 = f32[2,128,128]{1,2,0:T(8,128)S(1)} custom-call(f32[2,128,128]{2,1,0:T(8,128)S(1)} %get-tuple-element.86), custom_call_target="InvertDiagBlocksLowerTriangular" | custom-call | tf_op jit(solution)/shard_map/jit(_solve_triangular)/triangular_solve | solution.py:16
  180.1 39.8 %custom-call.45 = f32[4,128,128]{1,2,0:T(8,128)S(1)} custom-call(f32[4,128,128]{2,1,0:T(8,128)S(1)} %get-tuple-element.87), custom_call_target="InvertDiagBlocksLowerTriangular" | custom-call | tf_op jit(solution)/shard_map/jit(_solve_triangular)/triangular_solve | solution.py:16
  225.0 34.4 %all-gather.16.cloned.1.call-done = f32[2,512,512]{2,1,0:T(8,128)} async-done(((f32[2,512,128]{2,1,0:T(8,128)}), f32[2,512,512]{2,1,0:T(8,128)}) %all-gather.16.cloned.1.call-update) | async-done | bytes 2097168 | tf_op jit(solution)/shard_map/all_gather | solution.py:68
  280.2 27.9 %all-gather.18.cloned.1.call-done = f32[512,512]{0,1:T(8,128)} async-done(((f32[512,128]{0,1:T(8,128)}), f32[512,512]{0,1:T(8,128)}) %all-gather.18.cloned.1.call-update) | async-done | bytes 1048592 | tf_op jit(solution)/shard_map/all_gather | solution.py:33
  350.7 19.9 %custom-call.47 = f32[2,128,128]{1,2,0:T(8,128)S(1)} custom-call(f32[2,128,128]{2,1,0:T(8,128)S(1)} %get-tuple-element.88), custom_call_target="InvertDiagBlocksLowerTriangular" | custom-call | tf_op jit(solution)/shard_map/jit(_solve_triangular)/triangular_solve | solution.py:16
  417.4 39.7 %custom-call.49 = f32[4,128,128]{1,2,0:T(8,128)S(1)} custom-call(f32[4,128,128]{2,1,0:T(8,128)S(1)} %get-tuple-element.89), custom_call_target="InvertDiagBlocksLowerTriangular" | custom-call | tf_op jit(solution)/shard_map/jit(_solve_triangular)/triangular_solve | solution.py:16
  462.2 34.4 %all-gather.20.cloned.1.call-done = f32[2,512,512]{2,1,0:T(8,128)} async-done(((f32[2,512,128]{2,1,0:T(8,128)}), f32[2,512,512]{2,1,0:T(8,128)}) %all-gather.20.cloned.1.call-update) | async-done | bytes 2097168 | tf_op jit(solution)/shard_map/all_gather | solution.py:68
  524.9 26.7 %all-gather.22.cloned.1.call-done = f32[512,512]{0,1:T(8,128)} async-done(((f32[512,128]{0,1:T(8,128)}), f32[512,512]{0,1:T(8,128)}) %all-gather.22.cloned.1.call-update) | async-done | bytes 1048592 | tf_op jit(solution)/shard_map/all_gather | solution.py:33
  594.4 19.9 %custom-call.51 = f32[2,128,128]{1,2,0:T(8,128)S(1)} custom-call(f32[2,128,128]{2,1,0:T(8,128)S(1)} %get-tuple-element.90), custom_call_target="InvertDiagBlocksLowerTriangular" | custom-call | tf_op jit(solution)/shard_map/jit(_solve_triangular)/triangular_solve | solution.py:16
  661.0 39.7 %custom-call.53 = f32[4,128,128]{1,2,0:T(8,128)S(1)} custom-call(f32[4,128,128]{2,1,0:T(8,128)S(1)} %get-tuple-element.91), custom_call_target="InvertDiagBlocksLowerTriangular" | custom-call | tf_op jit(solution)/shard_map/jit(_solve_triangular)/triangular_solve | solution.py:16
  705.8 34.4 %all-gather.24.cloned.1.call-done = f32[2,512,512]{2,1,0:T(8,128)} async-done(((f32[2,512,128]{2,1,0:T(8,128)}), f32[2,512,512]{2,1,0:T(8,128)}) %all-gather.24.cloned.1.call-update) | async-done | bytes 2097168 | tf_op jit(solution)/shard_map/all_gather | solution.py:68
  785.1 24.6 %all-gather.26.cloned.1.call-done = f32[512,512]{0,1:T(8,128)} async-done(((f32[512,128]{0,1:T(8,128)}), f32[512,512]{0,1:T(8,128)}) %all-gather.26.cloned.1.call-update) | async-done | bytes 1048592 | tf_op jit(solution)/shard_map/all_gather | solution.py:33
  852.4 19.9 %custom-call.55 = f32[2,128,128]{1,2,0:T(8,128)S(1)} custom-call(f32[2,128,128]{2,1,0:T(8,128)S(1)} %get-tuple-element.92), custom_call_target="InvertDiagBlocksLowerTriangular" | custom-call | tf_op jit(solution)/shard_map/jit(_solve_triangular)/triangular_solve | solution.py:16
  919.1 39.7 %custom-call.57 = f32[4,128,128]{1,2,0:T(8,128)S(1)} custom-call(f32[4,128,128]{2,1,0:T(8,128)S(1)} %get-tuple-element.93), custom_call_target="InvertDiagBlocksLowerTriangular" | custom-call | tf_op jit(solution)/shard_map/jit(_solve_triangular)/triangular_solve | solution.py:16
  963.9 34.4 %all-gather.28.cloned.1.call-done = f32[2,512,512]{2,1,0:T(8,128)} async-done(((f32[2,512,128]{2,1,0:T(8,128)}), f32[2,512,512]{2,1,0:T(8,128)}) %all-gather.28.cloned.1.call-update) | async-done | bytes 2097168 | tf_op jit(solution)/shard_map/all_gather | solution.py:68
  1027.0 24.6 %all-gather.30.cloned.1.call-done = f32[512,512]{0,1:T(8,128)} async-done(((f32[512,128]{0,1:T(8,128)}), f32[512,512]{0,1:T(8,128)}) %all-gather.30.cloned.1.call-update) | async-done | bytes 1048592 | tf_op jit(solution)/shard_map/all_gather | solution.py:33
  1094.3 19.9 %custom-call.59 = f32[2,128,128]{1,2,0:T(8,128)S(1)} custom-call(f32[2,128,128]{2,1,0:T(8,128)S(1)} %get-tuple-element.94), custom_call_target="InvertDiagBlocksLowerTriangular" | custom-call | tf_op jit(solution)/shard_map/jit(_solve_triangular)/triangular_solve | solution.py:16
  1160.9 39.7 %custom-call.61 = f32[4,128,128]{1,2,0:T(8,128)S(1)} custom-call(f32[4,128,128]{2,1,0:T(8,128)S(1)} %get-tuple-element.95), custom_call_target="InvertDiagBlocksLowerTriangular" | custom-call | tf_op jit(solution)/shard_map/jit(_solve_triangular)/triangular_solve | solution.py:16
  1205.8 34.4 %all-gather.32.cloned.1.call-done = f32[2,512,512]{2,1,0:T(8,128)} async-done(((f32[2,512,128]{2,1,0:T(8,128)}), f32[2,512,512]{2,1,0:T(8,128)}) %all-gather.32.cloned.1.call-update) | async-done | bytes 2097168 | tf_op jit(solution)/shard_map/all_gather | solution.py:68
  1268.0 26.7 %all-gather.34.cloned.1.call-done = f32[512,512]{0,1:T(8,128)} async-done(((f32[512,128]{0,1:T(8,128)}), f32[512,512]{0,1:T(8,128)}) %all-gather.34.cloned.1.call-update) | async-done | bytes 1048592 | tf_op jit(solution)/shard_map/all_gather | solution.py:33
  1337.2 19.9 %custom-call.63 = f32[2,128,128]{1,2,0:T(8,128)S(1)} custom-call(f32[2,128,128]{2,1,0:T(8,128)S(1)} %get-tuple-element.96), custom_call_target="InvertDiagBlocksLowerTriangular" | custom-call | tf_op jit(solution)/shard_map/jit(_solve_triangular)/triangular_solve | solution.py:16
  1404.2 39.6 %custom-call.21 = f32[4,128,128]{1,2,0:T(8,128)S(1)} custom-call(f32[4,128,128]{2,1,0:T(8,128)S(1)} %get-tuple-element.31), custom_call_target="InvertDiagBlocksLowerTriangular" | custom-call | tf_op jit(solution)/shard_map/jit(_solve_triangular)/triangular_solve | solution.py:81
  (522 shorter events, 783.3 us)
Async XLA Ops:
  6.5 28.8 %all-gather.36.cloned.1.call-start = ((), (), s32[]{:S(2)}) async-start(), calls=%async_computation.11 | async-start | bytes 1310720 | tf_op jit(solution)/shard_map/all_gather | solution.py:46
  7.3 64.1 %all-gather.14.cloned.1.call-start = ((), (), s32[]{:S(2)}) async-start(), calls=%async_computation | async-start | bytes 1310720 | tf_op jit(solution)/shard_map/all_gather | solution.py:33
  37.8 5.8 collective-permute-start
  45.1 214.3 %all-gather.16.cloned.1.call-start = ((), (), s32[]{:S(2)}) async-start(), calls=%async_computation.1 | async-start | bytes 2621440 | tf_op jit(solution)/shard_map/all_gather | solution.py:68
  224.9 83.1 %all-gather.18.cloned.1.call-start = ((), (), s32[]{:S(2)}) async-start(), calls=%async_computation.2 | async-start | bytes 1310720 | tf_op jit(solution)/shard_map/all_gather | solution.py:33
  263.8 13.3 collective-permute-start.1
  265.8 13.1 collective-permute-start.2
  279.9 216.7 %all-gather.20.cloned.1.call-start = ((), (), s32[]{:S(2)}) async-start(), calls=%async_computation.3 | async-start | bytes 2621440 | tf_op jit(solution)/shard_map/all_gather | solution.py:68
  309.0 61.6 %copy-start.6 = (f32[512,512]{0,1:T(8,128)S(1)}, f32[512,512]{0,1:T(8,128)}, u32[]{:S(2)}) copy-start(f32[512,512]{0,1:T(8,128)} %all-gather.18.cloned.1.call-done) | copy-start | bytes 3145732
  462.1 89.5 %all-gather.22.cloned.1.call-start = ((), (), s32[]{:S(2)}) async-start(), calls=%async_computation.4 | async-start | bytes 1310720 | tf_op jit(solution)/shard_map/all_gather | solution.py:33
  501.0 19.8 %collective-permute-start.3 = (f32[512,384]{0,1:T(8,128)S(1)}, f32[512,384]{0,1:T(8,128)S(1)}, u32[]{:S(2)}, u32[]{:S(2)}) collective-permute-start(f32[512,384]{0,1:T(8,128)S(1)} %get-tuple-element.243), channel_id=1, source_target_pairs={{0,8},{4,12},{8,16},{12,20},{16,24},{20,28},{24,32},{28,36},{32,40... | collective-permute-start | bytes 2359304 | tf_op jit(solution)/shard_map/ppermute | solution.py:12
  504.1 19.5 %collective-permute-start.4 = (f32[512,384]{0,1:T(8,128)S(1)}, f32[512,384]{0,1:T(8,128)S(1)}, u32[]{:S(2)}, u32[]{:S(2)}) collective-permute-start(f32[512,384]{0,1:T(8,128)S(1)} %get-tuple-element.244), channel_id=1, source_target_pairs={{8,0},{12,4},{16,8},{20,12},{24,16},{28,20},{32,24},{36,28},{40,32... | collective-permute-start | bytes 2359304 | tf_op jit(solution)/shard_map/ppermute | solution.py:12
  524.6 215.6 %all-gather.24.cloned.1.call-start = ((), (), s32[]{:S(2)}) async-start(), calls=%async_computation.5 | async-start | bytes 2621440 | tf_op jit(solution)/shard_map/all_gather | solution.py:68
  705.8 103.9 %all-gather.26.cloned.1.call-start = ((), (), s32[]{:S(2)}) async-start(), calls=%async_computation.6 | async-start | bytes 1310720 | tf_op jit(solution)/shard_map/all_gather | solution.py:33
  744.7 21.3 %collective-permute-start.5 = (f32[512,384]{0,1:T(8,128)S(1)}, f32[512,384]{0,1:T(8,128)S(1)}, u32[]{:S(2)}, u32[]{:S(2)}) collective-permute-start(f32[512,384]{0,1:T(8,128)S(1)} %get-tuple-element.239), channel_id=1, source_target_pairs={{0,16},{4,20},{8,24},{12,28},{16,32},{20,36},{24,40},{28,44},{32,4... | collective-permute-start | bytes 2359304 | tf_op jit(solution)/shard_map/ppermute | solution.py:12
  748.1 35.7 %collective-permute-start.6 = (f32[512,384]{0,1:T(8,128)S(1)}, f32[512,384]{0,1:T(8,128)S(1)}, u32[]{:S(2)}, u32[]{:S(2)}) collective-permute-start(f32[512,384]{0,1:T(8,128)S(1)} %get-tuple-element.240), channel_id=1, source_target_pairs={{16,0},{20,4},{24,8},{28,12},{32,16},{36,20},{40,24},{44,28},{48,3... | collective-permute-start | bytes 2359304 | tf_op jit(solution)/shard_map/ppermute | solution.py:12
  784.8 213.4 %all-gather.28.cloned.1.call-start = ((), (), s32[]{:S(2)}) async-start(), calls=%async_computation.7 | async-start | bytes 2621440 | tf_op jit(solution)/shard_map/all_gather | solution.py:68
  963.8 87.8 %all-gather.30.cloned.1.call-start = ((), (), s32[]{:S(2)}) async-start(), calls=%async_computation.8 | async-start | bytes 1310720 | tf_op jit(solution)/shard_map/all_gather | solution.py:33
  1002.7 18.9 %collective-permute-start.7 = (f32[512,384]{0,1:T(8,128)S(1)}, f32[512,384]{0,1:T(8,128)S(1)}, u32[]{:S(2)}, u32[]{:S(2)}) collective-permute-start(f32[512,384]{0,1:T(8,128)S(1)} %get-tuple-element.235), channel_id=1, source_target_pairs={{0,32},{4,36},{8,40},{12,44},{16,48},{20,52},{24,56},{28,60},{32,6... | collective-permute-start | bytes 2359304 | tf_op jit(solution)/shard_map/ppermute | solution.py:12
  1006.2 19.5 %collective-permute-start.8 = (f32[512,384]{0,1:T(8,128)S(1)}, f32[512,384]{0,1:T(8,128)S(1)}, u32[]{:S(2)}, u32[]{:S(2)}) collective-permute-start(f32[512,384]{0,1:T(8,128)S(1)} %get-tuple-element.236), channel_id=1, source_target_pairs={{32,0},{36,4},{40,8},{44,12},{48,16},{52,20},{56,24},{60,28},{64,3... | collective-permute-start | bytes 2359304 | tf_op jit(solution)/shard_map/ppermute | solution.py:12
  1026.8 213.4 %all-gather.32.cloned.1.call-start = ((), (), s32[]{:S(2)}) async-start(), calls=%async_computation.9 | async-start | bytes 2621440 | tf_op jit(solution)/shard_map/all_gather | solution.py:68
  1205.7 89.0 %all-gather.34.cloned.1.call-start = ((), (), s32[]{:S(2)}) async-start(), calls=%async_computation.10 | async-start | bytes 1310720 | tf_op jit(solution)/shard_map/all_gather | solution.py:33
  1244.6 21.3 %collective-permute-start.10 = (f32[512,384]{0,1:T(8,128)S(1)}, f32[512,384]{0,1:T(8,128)S(1)}, u32[]{:S(2)}, u32[]{:S(2)}) collective-permute-start(f32[512,384]{0,1:T(8,128)S(1)} %get-tuple-element.232), channel_id=1, source_target_pairs={{64,0},{68,4},{72,8},{76,12},{80,16},{84,20},{88,24},{92,28},{96,3... | collective-permute-start | bytes 2359304 | tf_op jit(solution)/shard_map/ppermute | solution.py:12
  1245.9 21.2 %collective-permute-start.9 = (f32[512,384]{0,1:T(8,128)S(1)}, f32[512,384]{0,1:T(8,128)S(1)}, u32[]{:S(2)}, u32[]{:S(2)}) collective-permute-start(f32[512,384]{0,1:T(8,128)S(1)} %get-tuple-element.231), channel_id=1, source_target_pairs={{0,64},{4,68},{8,72},{12,76},{16,80},{20,84},{24,88},{28,92},{32,9... | collective-permute-start | bytes 2359304 | tf_op jit(solution)/shard_map/ppermute | solution.py:12
  (11 other events, 469.1 us)
Sparse Core Ops, SparseCore 0:
  9.0 26.2 all-gather.35
  45.2 26.0 all-gather.13
  225.1 34.2 all-gather.15
  280.0 27.9 all-gather.17
  462.2 34.2 all-gather.19
  524.8 26.8 all-gather.21
  705.9 34.2 all-gather.23
  785.0 24.7 all-gather.25
  964.0 34.2 all-gather.27
  1026.9 24.6 all-gather.29
  1205.8 34.2 all-gather.31
  1268.2 26.5 all-gather.33
where the time goes:
time: 1470 us; the launch traced here: 1460 us
  other arithmetic  792 us (54%)
  waiting for transfers between devices  452 us (31%)
  local copies, waits for them, and re-layouts  82.2 us (6%)
  matrix products  63.1 us (4%)
  starting transfers between devices  34.3 us (2%)
  between operations  31.4 us (2%)
    another operation x29, other arithmetic, solve_lower(): return jax.scipy.linalg.solve_triangular(factor, values, lower=True)  319 us
    another operation x42, other arithmetic, block_cholesky(): lower_right = jnp.linalg.cholesky(schur_part)  208 us
    another operation x41, other arithmetic, block_cholesky(): upper_left = jnp.linalg.cholesky(matrix[:half, :half])  207 us
    all_gather x5, waiting for transfers between devices, local(): lax.all_gather(stacked, 'row', axis=2, tiled=True)  172 us
    all_gather x6, waiting for transfers between devices, factor_split(): full_diag = lax.all_gather(diag_part, 'row', axis=1, tiled=True)  156 us
    ppermute x11, waiting for transfers between devices, passed_along(): return lax.ppermute(block, axis, route)  95 us
    another operation x116, local copies, waits for them, and re-layouts, solve_lower(): return jax.scipy.linalg.solve_triangular(factor, values, lower=True)  64.6 us
    another operation x2, other arithmetic, local(): jax.scipy.linalg.solve_triangular(factor, inner, lower=True, trans=1)  39.7 us
  transfers between devices with their start and end apart: 23, of which 23 were waited for; matrix products, arithmetic and copies ran while one was open for 0% of the time, Pallas kernels for 0%

commit v1 on v0

v1 whole, which is shorter than its diff:
```python
import functools

import jax
import jax.numpy as jnp
from jax import lax
from jax.experimental import pallas as pl
from jax.experimental.pallas import tpu as pltpu
from jax.sharding import PartitionSpec as P

MESH = pl.DeviceIdType.MESH
EXACT = lax.Precision.HIGHEST
Q = 128
G = 8


def dot(a, b, ca=1, cb=0):
    return lax.dot_general(
        a, b, (((ca,), (cb,)), ((), ())), precision=EXACT, preferred_element_type=jnp.float32
    )


def lanes(v, k):
    return jnp.broadcast_to(v[:, k : k + 1], v.shape)


def subs(v, k):
    return jnp.broadcast_to(v[k : k + 1, :], v.shape)


def inverse_factor(rows):
    lane = lax.broadcasted_iota(jnp.int32, (G, Q), 1)
    sub = lax.broadcasted_iota(jnp.int32, (G, Q), 0)
    rows = list(rows)
    count = len(rows)
    out = []
    for g in range(count):
        c0 = G * g
        inside = (lane >= c0) & (lane < c0 + G)
        cols = [lanes(rows[g], c0 + k) for k in range(G)]
        v = jnp.where(inside, jnp.where(lane == sub + c0, 1.0, 0.0), rows[g])
        inv, upper = [], {}
        scale = jnp.ones((G, Q), jnp.float32)
        for k in range(G):
            pivot = subs(cols[k], k)
            inv.append(1.0 / pivot)
            scale = jnp.where(sub == k, lax.rsqrt(pivot), scale)
            if k < G - 1:
                m = jnp.where(sub > k, cols[k] * inv[k], 0.0)
                for k2 in range(k + 1, G):
                    upper[k, k2] = subs(cols[k2], k)
                    cols[k2] = cols[k2] - m * upper[k, k2]
                v = v - m * subs(v, k)
        spread = [subs(v, k) for k in range(G)]
        for h in range(g + 1, count):
            below = [lanes(rows[h], c0 + k) for k in range(G)]
            w = jnp.where(inside, 0.0, rows[h])
            for k in range(G):
                m = below[k] * inv[k]
                for k2 in range(k + 1, G):
                    below[k2] = below[k2] - m * upper[k, k2]
                w = w - m * spread[k]
            rows[h] = w
        out.append(jnp.where(lane <= sub + c0, v * scale, 0.0))
    return out


def side(blocks):
    return jnp.concatenate(blocks, axis=1)


def factorize(a, panel):
    tiles = a.shape[0]

    def step(j, carry):
        here = pl.ds(pl.multiple_of(j * Q, Q), Q)
        rows = [a[j, pl.ds(pl.multiple_of(j * Q + G * h, G), G), :] for h in range(Q // G)]
        top = jnp.concatenate(inverse_factor(rows), axis=0)
        across = dot(top, side([a[c, here, :] for c in range(tiles)]))
        for c in range(tiles):
            block = jnp.where(c == j, top, across[:, c * Q : (c + 1) * Q])
            panel[c] = block
            a[c, here, :] = jnp.where(c <= j, block, 0.0)
        for i in range(1, tiles):

            @pl.when(i > j)
            def _():
                there = slice(i * Q, (i + 1) * Q)
                update = dot(panel[i], side([panel[c] for c in range(tiles)]), 0, 0)
                for c in range(tiles):
                    old = jnp.where(c == j, 0.0, a[c, there, :])
                    a[c, there, :] = old - update[:, c * Q : (c + 1) * Q]

        return carry

    lax.fori_loop(0, tiles, step, 0)


def kernel(blocks, levels, f_ref, mass_ref, rhs_ref, out_ref, a, panel, w, rcur, fown, fnext, massg, dg, lg, ug, dr, rr, staged,
           fsend, frecv, nsend, nrecv, msend, mrecv, send, recv):
    t = lax.axis_index("tm")
    r = lax.axis_index("row")
    tiles = a.shape[0]

    def peer(d):
        return (t, lax.rem(r + d, tiles))

    def source(d):
        return lax.rem(r + tiles - d, tiles)

    def copy(src, dst, ssem, rsem, device):
        return pltpu.make_async_remote_copy(
            src_ref=src, dst_ref=dst, send_sem=ssem, recv_sem=rsem, device_id=device, device_id_type=MESH
        )

    barrier = pltpu.get_barrier_semaphore()
    expected = tiles - 1
    for d in range(1, tiles):
        pl.semaphore_signal(barrier, inc=1, device_id=peer(d), device_id_type=MESH)
    for level in range(levels):
        s = 2**level
        up, down = t + s < blocks, t >= s

        @pl.when(up)
        def _():
            pl.semaphore_signal(barrier, inc=1, device_id=(t + s, r), device_id_type=MESH)

        @pl.when(down)
        def _():
            pl.semaphore_signal(barrier, inc=1, device_id=(t - s, r), device_id_type=MESH)

        expected = expected + up.astype(jnp.int32) + down.astype(jnp.int32)
    pl.semaphore_wait(barrier, expected)

    def f_copy(d):
        return copy(f_ref, fown.at[r], fsend.at[d - 1], frecv.at[d - 1], peer(d))

    def f_arrived(d):
        return copy(f_ref, fown.at[source(d)], fsend.at[d - 1], frecv.at[d - 1], peer(d))

    def m_copy(d):
        return copy(mass_ref, massg.at[r], msend.at[d - 1], mrecv.at[d - 1], peer(d))

    def m_arrived(d):
        return copy(mass_ref, massg.at[source(d)], msend.at[d - 1], mrecv.at[d - 1], peer(d))

    def n_copy(d):
        src = f_ref if d == 0 else fown.at[source(d)]
        return copy(src, fnext.at[source(d)], nsend.at[d], nrecv.at[d], (t - 1, r))

    order = (1, 3, 2)
    for d in order:
        f_copy(d).start()
    for d in order:
        m_copy(d).start()

    @pl.when(t >= 1)
    def _():
        n_copy(0).start()

    fown[r] = f_ref[...]
    massg[r] = mass_ref[...]
    rcur[...] = rhs_ref[...]
    for d in order:
        f_arrived(d).wait_recv()

        @pl.when(t >= 1)
        def _():
            n_copy(d).start()

    for d in order:
        m_arrived(d).wait_recv()

    row_ids = lax.broadcasted_iota(jnp.int32, (tiles * Q, Q), 0)
    col_ids = lax.broadcasted_iota(jnp.int32, (tiles * Q, Q), 1)

    def own_gram(p, carry):
        full = fown[...].reshape(tiles * Q, tiles * Q)
        pair = fown[pl.ds(2 * p, 2)].reshape(2 * Q, tiles * Q)
        gram = dot(full, pair, 1, 1)
        for e in range(2):
            c = 2 * p + e
            block = gram[:, e * Q : (e + 1) * Q]
            lg[0, c] = -block
            dg[0, c] = block + jnp.where(row_ids == col_ids + c * Q, massg[c], 0.0)
        return carry

    lax.fori_loop(0, tiles // 2, own_gram, 0)

    @pl.when(t + 1 < blocks)
    def _():
        for d in (0,) + order:
            n_copy(d).wait_recv()

        def next_gram(p, carry):
            full = fnext[...].reshape(tiles * Q, tiles * Q)
            pair = fnext[pl.ds(2 * p, 2)].reshape(2 * Q, tiles * Q)
            gram = dot(full, pair, 1, 1)
            for e in range(2):
                c = 2 * p + e
                block = gram[:, e * Q : (e + 1) * Q]
                ug[0, c] = -block
                dg[0, c] = dg[0, c] + block
            return carry

        lax.fori_loop(0, tiles // 2, next_gram, 0)

    for d in order:
        f_copy(d).wait_send()
        m_copy(d).wait_send()

    @pl.when(t >= 1)
    def _():
        for d in (0,) + order:
            n_copy(d).wait_send()

    def along(i, s, k):
        device = (t + s, r) if k % 2 == 0 else (t - s, r)
        target = {0: dr, 1: dr, 4: rr, 5: rr}.get(k)
        if target is not None:
            dst = target.at[i, k % 2]
        else:
            dst = (lg if k == 2 else ug).at[i + 1, r]
        return copy(staged.at[i, k], dst, send.at[i, k], recv.at[i, k], device)

    def across_row(i, k, d, slot):
        buffer = (dg, lg, ug)[k]
        sem = 6 + 3 * k + d - 1
        return copy(buffer.at[i + 1, r], buffer.at[i + 1, slot], send.at[i, sem], recv.at[i, sem], peer(d))

    def take_rhs(i, s):
        @pl.when(t >= s)
        def _():
            along(i, s, 4).wait_recv()
            rcur[...] = rcur[...] - rr[i, 0]

        @pl.when(t + s < blocks)
        def _():
            along(i, s, 5).wait_recv()
            rcur[...] = rcur[...] - rr[i, 1]

    def gather_arrived(i, k):
        for d in order:
            across_row(i, k, d, source(d)).wait_recv()

    def whiten(src, i, base):
        def pair(p, carry):
            inverse = side([a[c] for c in range(tiles)])
            both = dot(inverse, side([src[i, 2 * p], src[i, 2 * p + 1]]))
            w[base + 2 * p] = both[:, :Q]
            w[base + 2 * p + 1] = both[:, Q:]
            return carry

        lax.fori_loop(0, tiles // 2, pair, 0)

    def level(i, s):
        up, down = t + s < blocks, t >= s
        for c in range(tiles):
            a[c] = dg[i, c]
        factorize(a, panel)

        @pl.when(i > 0)
        def _():
            take_rhs(i - 1, s // 2)

        @pl.when(down & (i > 0))
        def _():
            gather_arrived(i - 1, 1)

        @pl.when(up & (i > 0))
        def _():
            gather_arrived(i - 1, 2)

        @pl.when(up)
        def _():
            whiten(ug, i, tiles)
            later = side([w[tiles + c] for c in range(tiles)])
            staged[i, 0] = dot(later, w[tiles + r], 0, 0)
            along(i, s, 0).start()

        @pl.when(down)
        def _():
            whiten(lg, i, 0)
            earlier = side([w[c] for c in range(tiles)])
            staged[i, 1] = dot(earlier, w[r], 0, 0)
            along(i, s, 1).start()

        @pl.when(up & down)
        def _():
            later = side([w[tiles + c] for c in range(tiles)])
            staged[i, 2] = -dot(later, w[r], 0, 0)
            along(i, s, 2).start()
            earlier = side([w[c] for c in range(tiles)])
            staged[i, 3] = -dot(earlier, w[tiles + r], 0, 0)
            along(i, s, 3).start()

        w[2 * tiles] = dot(side([a[c] for c in range(tiles)]), rcur[...])

        @pl.when(up)
        def _():
            later = side([w[tiles + c] for c in range(tiles)])
            staged[i, 4] = dot(later, w[2 * tiles], 0, 0)
            along(i, s, 4).start()

        @pl.when(down)
        def _():
            earlier = side([w[c] for c in range(tiles)])
            staged[i, 5] = dot(earlier, w[2 * tiles], 0, 0)
            along(i, s, 5).start()

        @pl.when(i < levels)
        def _():
            dg[i + 1, r] = dg[i, r]

            @pl.when(down)
            def _():
                along(i, s, 0).wait_recv()
                dg[i + 1, r] = dg[i + 1, r] - dr[i, 0]

            @pl.when(up)
            def _():
                along(i, s, 1).wait_recv()
                dg[i + 1, r] = dg[i + 1, r] - dr[i, 1]

            for d in order:
                across_row(i, 0, d, r).start()

            @pl.when(t >= 2 * s)
            def _():
                along(i, s, 2).wait_recv()
                for d in order:
                    across_row(i, 1, d, r).start()

            @pl.when(t + 2 * s < blocks)
            def _():
                along(i, s, 3).wait_recv()
                for d in order:
                    across_row(i, 2, d, r).start()

            gather_arrived(i, 0)

        return s * 2

    lax.fori_loop(0, levels + 1, level, 1)
    out_ref[...] = dot(side([a[c] for c in range(tiles)]), w[2 * tiles], 0, 0)

    def drain(i, s):
        up, down = t + s < blocks, t >= s

        @pl.when(up)
        def _():
            along(i, s, 0).wait_send()
            along(i, s, 4).wait_send()

        @pl.when(down)
        def _():
            along(i, s, 1).wait_send()
            along(i, s, 5).wait_send()

        @pl.when(up & down)
        def _():
            along(i, s, 2).wait_send()
            along(i, s, 3).wait_send()

        for d in order:
            across_row(i, 0, d, r).wait_send()

        @pl.when(t >= 2 * s)
        def _():
            for d in order:
                across_row(i, 1, d, r).wait_send()

        @pl.when(t + 2 * s < blocks)
        def _():
            for d in order:
                across_row(i, 2, d, r).wait_send()

        return s * 2

    lax.fori_loop(0, levels, drain, 1)


def local(edge_factor, mass, rhs):
    blocks = lax.axis_size("tm")
    tiles = lax.axis_size("row")
    levels = (blocks - 1).bit_length()
    quarter, nodes = edge_factor.shape[1:]
    f32 = jnp.float32
    vmem = pl.BlockSpec(memory_space=pltpu.VMEM)
    dma = pltpu.SemaphoreType.DMA
    column = (nodes, quarter)
    mass_rows = jnp.broadcast_to(mass, (1, quarter))
    result = pl.pallas_call(
        functools.partial(kernel, blocks, levels),
        out_shape=jax.ShapeDtypeStruct(column, f32),
        in_specs=[vmem] * 3,
        out_specs=vmem,
        scratch_shapes=[
            pltpu.VMEM((tiles,) + column, f32),
            pltpu.VMEM((tiles, quarter, quarter), f32),
            pltpu.VMEM((2 * tiles + 1,) + column, f32),
            pltpu.VMEM(column, f32),
            pltpu.VMEM((tiles, quarter, nodes), f32),
            pltpu.VMEM((tiles, quarter, nodes), f32),
            pltpu.VMEM((tiles, 1, quarter), f32),
            pltpu.VMEM((levels + 1, tiles) + column, f32),
            pltpu.VMEM((levels + 1, tiles) + column, f32),
            pltpu.VMEM((levels + 1, tiles) + column, f32),
            pltpu.VMEM((levels, 2) + column, f32),
            pltpu.VMEM((levels, 2) + column, f32),
            pltpu.VMEM((levels, 6) + column, f32),
            dma((3,)), dma((3,)), dma((4,)), dma((4,)), dma((3,)), dma((3,)),
            dma((levels, 15)), dma((levels, 15)),
        ],
        compiler_params=pltpu.CompilerParams(
            collective_id=0, has_side_effects=True, vmem_limit_bytes=63 * 1024 * 1024
        ),
    )(edge_factor[0], mass_rows, rhs[0])
    return result[None]


def solution(mesh):
    placed = (P("tm", "row", None), P("tm", "row"), P("tm", None, "row"))
    return jax.shard_map(
        local, mesh=mesh, in_specs=placed, out_specs=P("tm", None, "row"), check_vma=False
    )
```

time: 1470 us -> 298 us (0.20)
  other arithmetic: 792 us -> 0 us
  waiting for transfers between devices: 452 us -> 0 us
  Pallas kernels: 0 us -> 294 us
  local copies, waits for them, and re-layouts: 82.2 us -> 1.67 us
  matrix products: 63.1 us -> 0 us
  starting transfers between devices: 34.3 us -> 0 us
  between operations: 31.4 us -> 0.01 us
    another operation x119 -> x0, other arithmetic: 778 us -> none  [the longest x29 319 us: solve_lower(): return jax.scipy.linalg.solve_triangular(factor, values, lower=True)]
    all_gather x12 -> x0, waiting for transfers between devices: 356 us -> none  [the longest x5 172 us: local(): lax.all_gather(stacked, 'row', axis=2, tiled=True)]
    pallas_call x0 -> x1, Pallas kernels: none -> 294 us  [local(): pl.pallas_call(functools.partial(kernel, blocks, levels), out_shape=jax.S...]
    ppermute x11 -> x0, waiting for transfers between devices: 95 us -> none  [passed_along(): return lax.ppermute(block, axis, route)]
    another operation x169 -> x0, local copies, waits for them, and re-layouts: 74 us -> none  [the longest x116 64.6 us: solve_lower(): return jax.scipy.linalg.solve_triangular(factor, values, lower=True)]
    another operation x91 -> x0, matrix products: 36.5 us -> none  [the longest x60 28.3 us: solve_lower(): return jax.scipy.linalg.solve_triangular(factor, values, lower=True)]
    ppermute x11 -> x0, starting transfers between devices: 33.1 us -> none  [passed_along(): return lax.ppermute(block, axis, route)]
    dot_general x12 -> x0, matrix products: 26.5 us -> none  [the longest x5 21.6 us: local(): jnp.einsum('tbn,bk->tnk', lax.all_gather(stacked, 'row', axis=2, tiled=Tr...]
  transfers between devices with their start and end apart: 23 -> 0, of which waited for: 23 -> 0; matrix products, arithmetic and copies ran while one was open for 0% -> 0% of each run, Pallas kernels for 0% -> 0%
where the time goes in v1:
time: 298 us; the launch traced here: 296 us
  Pallas kernels  294 us (99%)
    pallas_call x1, Pallas kernels, local(): pl.pallas_call(functools.partial(kernel, blocks, levels), out_shape=jax.S...  294 us

profile of v1, /device:TPU:16, one launch (start us, length us, event | category | flops | bytes accessed | tf_op | source)
XLA Modules:
  0.0 295.6 jit_solution(12263131487490631041)
XLA Ops:
  0.0 293.9 %shard_map.37 = f32[512,128]{1,0:T(8,128)} custom-call(f32[128,512]{1,0:T(8,128)} %bitcast.4, f32[1,128]{1,0:T(1,128)} %mass_ref.1, f32[512,128]{1,0:T(8,128)} %bitcast.5), custom_call_target="tpu_custom_call" | custom-call | tf_op jit(solution)/shard_map/pallas_call | solution.py:392
  293.9 1.7 copy.5

commit v2 on v1

v2 whole, which is shorter than its diff:
```python
import functools

import jax
import jax.numpy as jnp
from jax import lax
from jax.experimental import pallas as pl
from jax.experimental.pallas import tpu as pltpu
from jax.sharding import PartitionSpec as P

MESH = pl.DeviceIdType.MESH
EXACT = lax.Precision.HIGHEST
Q = 128
SPREAD = (0, 1)
G = 8


def dot(a, b, ca=1, cb=0):
    return lax.dot_general(
        a, b, (((ca,), (cb,)), ((), ())), precision=EXACT, preferred_element_type=jnp.float32
    )


def lanes(v, k):
    return jnp.broadcast_to(v[:, k : k + 1], v.shape)


def subs(v, k):
    return jnp.broadcast_to(v[k : k + 1, :], v.shape)


def eliminate(rows, base):
    lane = lax.broadcasted_iota(jnp.int32, (G, Q), 1)
    sub = lax.broadcasted_iota(jnp.int32, (G, Q), 0)
    rows = list(rows)
    count = len(rows)
    out = []
    cols = [lanes(rows[0], base + k) for k in range(G)]
    for g in range(count):
        c0 = base + G * g
        inside = (lane >= c0) & (lane < c0 + G)
        more = g + 1 < count
        if more:
            near = [lanes(rows[g + 1], c0 + k) for k in range(G)]
            after = [lanes(rows[g + 1], c0 + G + k) for k in range(G)]
            w = jnp.where(inside, 0.0, rows[g + 1])
        v = jnp.where(inside, jnp.where(lane == sub + c0, 1.0, 0.0), rows[g])
        inv, upper = [], {}
        scale = jnp.ones((G, Q), jnp.float32)
        for k in range(G):
            pivot = subs(cols[k], k)
            inv.append(1.0 / pivot)
            scale = jnp.where(sub == k, lax.rsqrt(pivot), scale)
            for k2 in range(k + 1, G):
                upper[k, k2] = subs(cols[k2], k)
            row = subs(v, k)
            if k < G - 1:
                m = jnp.where(sub > k, cols[k] * inv[k], 0.0)
                for k2 in range(k + 1, G):
                    cols[k2] = cols[k2] - m * upper[k, k2]
                v = v - m * row
            if more:
                m = near[k] * inv[k]
                for k2 in range(G):
                    after[k2] = after[k2] - m * subs(near[k], k2)
                for k2 in range(k + 1, G):
                    near[k2] = near[k2] - m * upper[k, k2]
                w = w - m * row
        if more:
            rows[g + 1] = w
            cols = after
        spread = [subs(v, k) for k in range(G)]
        for h in range(g + 2, count):
            below = [lanes(rows[h], c0 + k) for k in range(G)]
            w = jnp.where(inside, 0.0, rows[h])
            for k in range(G):
                m = below[k] * inv[k]
                for k2 in range(k + 1, G):
                    below[k2] = below[k2] - m * upper[k, k2]
                w = w - m * spread[k]
            rows[h] = w
        out.append(v * scale)
    return out


def inverse_factor(rows):
    lane = lax.broadcasted_iota(jnp.int32, (G, Q), 1)
    sub = lax.broadcasted_iota(jnp.int32, (G, Q), 0)
    half, middle = len(rows) // 2, Q // 2
    top = eliminate(rows[:half], 0)
    kept = [jnp.where((lane <= sub + G * g) | (lane >= middle), top[g], 0.0) for g in range(half)]
    stacked = jnp.concatenate(kept, axis=0)
    update = dot(stacked, stacked, 0, 0)
    rest = [jnp.where(lane < middle, 0.0, rows[h]) - update[G * h : G * h + G] for h in range(half, 2 * half)]
    both = top + eliminate(rest, middle)
    return [jnp.where(lane <= sub + G * g, both[g], 0.0) for g in range(2 * half)]


def side(blocks):
    return jnp.concatenate(blocks, axis=1)


def factorize(diag, inverse, upper, before, after):
    tiles = diag.shape[0]

    def step(j, carry):
        here = pl.ds(pl.multiple_of(j * Q, Q), Q)
        before(j)
        for c in range(tiles):
            inverse[c, here, :] = jnp.where(c < j, 0.0, diag[c, here, :])
        for above in range(1, tiles):

            @pl.when(j == above)
            def _():
                rows = slice(0, above * Q)
                known = [(inverse if c < above else upper)[c, rows, :] for c in range(tiles)]
                update = dot(upper[above, rows, :], side(known), 0, 0)
                for c in range(tiles):
                    inverse[c, here, :] = inverse[c, here, :] - update[:, c * Q : (c + 1) * Q]

        rows = [inverse[j, pl.ds(pl.multiple_of(j * Q + G * h, G), G), :] for h in range(Q // G)]
        top = jnp.concatenate(inverse_factor(rows), axis=0)
        across = dot(top, side([inverse[c, here, :] for c in range(tiles)]))
        for c in range(tiles):
            block = across[:, c * Q : (c + 1) * Q]
            upper[c, here, :] = block
            inverse[c, here, :] = jnp.where(c == j, top, jnp.where(c < j, block, 0.0))
        after(j)
        return carry

    lax.fori_loop(0, tiles, step, 0)


def kernel(blocks, levels, f_ref, mass_ref, rhs_ref, out_ref, a, upper, w, rcur, fown, fnext, massg, dg, lg, ug, dr, rr, staged, pairs,
           fsend, frecv, nsend, nrecv, msend, mrecv, send, recv):
    t = lax.axis_index("tm")
    r = lax.axis_index("row")
    tiles = a.shape[0]

    def peer(d):
        return (t, lax.rem(r + d, tiles))

    def source(d):
        return lax.rem(r + tiles - d, tiles)

    def copy(src, dst, ssem, rsem, device):
        return pltpu.make_async_remote_copy(
            src_ref=src, dst_ref=dst, send_sem=ssem, recv_sem=rsem, device_id=device, device_id_type=MESH
        )

    barrier = pltpu.get_barrier_semaphore()
    expected = tiles - 1
    for d in range(1, tiles):
        pl.semaphore_signal(barrier, inc=1, device_id=peer(d), device_id_type=MESH)
    for level in range(levels):
        s = 2**level
        up, down = t + s < blocks, t >= s

        @pl.when(up)
        def _():
            pl.semaphore_signal(barrier, inc=1, device_id=(t + s, r), device_id_type=MESH)

        @pl.when(down)
        def _():
            pl.semaphore_signal(barrier, inc=1, device_id=(t - s, r), device_id_type=MESH)

        expected = expected + up.astype(jnp.int32) + down.astype(jnp.int32)
    pl.semaphore_wait(barrier, expected)

    def f_copy(d):
        return copy(f_ref, fown.at[r], fsend.at[d - 1], frecv.at[d - 1], peer(d))

    def f_arrived(d):
        return copy(f_ref, fown.at[source(d)], fsend.at[d - 1], frecv.at[d - 1], peer(d))

    def f_on(d, slot):
        half = pl.ds(0 if d == 1 else Q // 2, Q // 2)
        sem = 1 if d == 1 else 3
        return copy(fown.at[slot, half], fown.at[slot, half], fsend.at[sem], frecv.at[sem], peer(d))

    def m_copy(d):
        return copy(mass_ref, massg.at[r], msend.at[d - 1], mrecv.at[d - 1], peer(d))

    def m_arrived(d):
        return copy(mass_ref, massg.at[source(d)], msend.at[d - 1], mrecv.at[d - 1], peer(d))

    def n_copy(d):
        src = f_ref if d == 0 else fown.at[source(d)]
        return copy(src, fnext.at[source(d)], nsend.at[d], nrecv.at[d], (t - 1, r))

    order = (1, 3, 2)
    for d in (1, 3):
        f_copy(d).start()
    for d in order:
        m_copy(d).start()

    @pl.when(t >= 1)
    def _():
        n_copy(0).start()

    fown[r] = f_ref[...]
    massg[r] = mass_ref[...]
    rcur[...] = rhs_ref[...]
    for d in (1, 3):
        f_arrived(d).wait_recv()
        f_on(d, source(d)).start()

        @pl.when(t >= 1)
        def _():
            n_copy(d).start()

    for d in (1, 3):
        f_on(d, source(2)).wait_recv()

    @pl.when(t >= 1)
    def _():
        n_copy(2).start()

    for d in order:
        m_arrived(d).wait_recv()

    row_ids = lax.broadcasted_iota(jnp.int32, (tiles * Q, Q), 0)
    col_ids = lax.broadcasted_iota(jnp.int32, (tiles * Q, Q), 1)

    def own_gram(p, carry):
        full = fown[...].reshape(tiles * Q, tiles * Q)
        pair = fown[pl.ds(2 * p, 2)].reshape(2 * Q, tiles * Q)
        gram = dot(full, pair, 1, 1)
        for e in range(2):
            c = 2 * p + e
            block = gram[:, e * Q : (e + 1) * Q]
            lg[0, c] = -block
            dg[0, c] = block + jnp.where(row_ids == col_ids + c * Q, massg[c], 0.0)
        return carry

    lax.fori_loop(0, tiles // 2, own_gram, 0)

    @pl.when(t + 1 < blocks)
    def _():
        for d in (0,) + order:
            n_copy(d).wait_recv()

        def next_gram(p, carry):
            full = fnext[...].reshape(tiles * Q, tiles * Q)
            pair = fnext[pl.ds(2 * p, 2)].reshape(2 * Q, tiles * Q)
            gram = dot(full, pair, 1, 1)
            for e in range(2):
                c = 2 * p + e
                block = gram[:, e * Q : (e + 1) * Q]
                ug[0, c] = -block
                dg[0, c] = dg[0, c] + block
            return carry

        lax.fori_loop(0, tiles // 2, next_gram, 0)

    for d in (1, 3):
        f_copy(d).wait_send()
        f_on(d, source(d)).wait_send()
    for d in order:
        m_copy(d).wait_send()

    @pl.when(t >= 1)
    def _():
        for d in (0,) + order:
            n_copy(d).wait_send()

    def along(i, s, k, c=None):
        device = (t + s, r) if k % 2 == 0 else (t - s, r)
        if k < 2:
            rows = pl.ds(c * Q, Q)
            src, dst, sem = staged.at[i, k, rows], dr.at[i, k, rows], 4 * k + c
        elif k < 4:
            src, dst, sem = pairs.at[i, k - 2, c], (lg if k == 2 else ug).at[i + 1, lax.rem(r + c, tiles)], 6 + 2 * k + c
        else:
            src, dst, sem = staged.at[i, k - 2], rr.at[i, k % 2], 10 + k
        return copy(src, dst, send.at[i, sem], recv.at[i, sem], device)

    def rows_across(i, c, d, slot):
        rows = pl.ds(c * Q, Q)
        sem = 16 + 3 * c + d - 1
        return copy(dg.at[i + 1, r, rows], dg.at[i + 1, slot, rows], send.at[i, sem], recv.at[i, sem], peer(d))

    def coupling_across(i, k, d):
        buffer = (lg, ug)[k]
        slot = r if d == 1 else lax.rem(r + 1, tiles)
        sem = 28 + 2 * k + (0 if d == 1 else 1)
        return copy(buffer.at[i + 1, slot], buffer.at[i + 1, slot], send.at[i, sem], recv.at[i, sem], peer(d))

    def coupling_arrives(i, k, d):
        buffer = (lg, ug)[k]
        slot = lax.rem(r + (3 if d == 1 else 2), tiles)
        sem = 28 + 2 * k + (0 if d == 1 else 1)
        return copy(buffer.at[i + 1, slot], buffer.at[i + 1, slot], send.at[i, sem], recv.at[i, sem], peer(d))

    def couples(i, s, k):
        return (t >= 2 * s) if k == 0 else (t + 2 * s < blocks)

    def take_rows(i, s, c):
        rows = slice(c * Q, (c + 1) * Q)
        dg[i + 1, r, rows] = dg[i, r, rows]

        @pl.when(t >= s)
        def _():
            along(i, s, 0, c).wait_recv()
            dg[i + 1, r, rows] = dg[i + 1, r, rows] - dr[i, 0, rows]

        @pl.when(t + s < blocks)
        def _():
            along(i, s, 1, c).wait_recv()
            dg[i + 1, r, rows] = dg[i + 1, r, rows] - dr[i, 1, rows]

        for d in order:
            rows_across(i, c, d, r).start()

    def spread_couplings(i, s, k):
        @pl.when(couples(i, s, k))
        def _():
            for c in range(2):
                along(i, s, 2 + k, c).wait_recv()
            for d in (1, 3):
                coupling_across(i, k, d).start()

    def couplings_arrived(i, s, k):
        @pl.when(couples(i, s, k))
        def _():
            for d in (1, 3):
                coupling_arrives(i, k, d).wait_recv()

    def take_rhs(i, s):
        @pl.when(t >= s)
        def _():
            along(i, s, 4).wait_recv()
            rcur[...] = rcur[...] - rr[i, 0]

        @pl.when(t + s < blocks)
        def _():
            along(i, s, 5).wait_recv()
            rcur[...] = rcur[...] - rr[i, 1]

    def under(values):
        half = tiles // 2
        cut = half * Q
        upper_half = dot(side([a[c, :cut, :] for c in range(half)]), values[:cut])
        lower_half = dot(side([a[c, cut:, :] for c in range(tiles)]), values)
        return jnp.concatenate([upper_half, lower_half], axis=0)

    def whiten(src, i, base, p):
        first, second = lax.rem(r + 2 * p, tiles), lax.rem(r + 2 * p + 1, tiles)
        both = under(side([src[i, first], src[i, second]]))
        w[base + first] = both[:, :Q]
        w[base + second] = both[:, Q:]

    def level(i, s):
        up, down = t + s < blocks, t >= s
        past, reach = i - 1, s // 2

        def before(j):
            @pl.when(i > 0)
            def _():
                @pl.when(j == 0)
                def _():
                    take_rows(past, reach, 0)
                    take_rows(past, reach, 1)

                for d in order:
                    for c in range(tiles):

                        @pl.when(j == c)
                        def _():
                            rows_across(past, c, d, source(d)).wait_recv()

        def after(j):
            @pl.when(i > 0)
            def _():
                @pl.when(j == 0)
                def _():
                    take_rows(past, reach, 2)
                    take_rows(past, reach, 3)

                for k in range(2):

                    @pl.when(j == SPREAD[k])
                    def _():
                        spread_couplings(past, reach, k)

        factorize(dg.at[i], a, upper, before, after)

        @pl.when(up)
        def _():
            whiten(ug, i, tiles, 0)

        @pl.when(down)
        def _():
            whiten(lg, i, 0, 0)

        @pl.when(i > 0)
        def _():
            take_rhs(past, reach)

        w[2 * tiles] = under(rcur[...])

        @pl.when(i > 0)
        def _():
            couplings_arrived(past, reach, 0)
            couplings_arrived(past, reach, 1)

        @pl.when(up)
        def _():
            whiten(ug, i, tiles, 1)
            later = side([w[tiles + c] for c in range(tiles)])
            terms = dot(later, side([w[tiles + r], w[2 * tiles]]), 0, 0)
            staged[i, 0] = terms[:, :Q]
            staged[i, 2] = terms[:, Q:]
            for c in range(tiles):
                along(i, s, 0, c).start()

        @pl.when(down)
        def _():
            whiten(lg, i, 0, 1)
            earlier = side([w[c] for c in range(tiles)])
            terms = dot(earlier, side([w[r], w[2 * tiles]]), 0, 0)
            staged[i, 1] = terms[:, :Q]
            staged[i, 3] = terms[:, Q:]
            for c in range(tiles):
                along(i, s, 1, c).start()

        @pl.when(up & down)
        def _():
            second = lax.rem(r + 1, tiles)
            later = side([w[tiles + c] for c in range(tiles)])
            product = -dot(later, side([w[r], w[second]]), 0, 0)
            for c in range(2):
                pairs[i, 0, c] = product[:, c * Q : (c + 1) * Q]
                along(i, s, 2, c).start()
            earlier = side([w[c] for c in range(tiles)])
            product = -dot(earlier, side([w[tiles + r], w[tiles + second]]), 0, 0)
            for c in range(2):
                pairs[i, 1, c] = product[:, c * Q : (c + 1) * Q]
                along(i, s, 3, c).start()

        @pl.when(up)
        def _():
            along(i, s, 4).start()

        @pl.when(down)
        def _():
            along(i, s, 5).start()

        return s * 2

    lax.fori_loop(0, levels + 1, level, 1)
    out_ref[...] = dot(side([a[c] for c in range(tiles)]), w[2 * tiles], 0, 0)

    def drain(i, s):
        up, down = t + s < blocks, t >= s

        @pl.when(up)
        def _():
            for c in range(tiles):
                along(i, s, 0, c).wait_send()
            along(i, s, 4).wait_send()

        @pl.when(down)
        def _():
            for c in range(tiles):
                along(i, s, 1, c).wait_send()
            along(i, s, 5).wait_send()

        @pl.when(up & down)
        def _():
            for c in range(2):
                along(i, s, 2, c).wait_send()
                along(i, s, 3, c).wait_send()

        for c in range(tiles):
            for d in order:
                rows_across(i, c, d, r).wait_send()
        for k in range(2):

            @pl.when(couples(i, s, k))
            def _():
                for d in (1, 3):
                    coupling_across(i, k, d).wait_send()

        return s * 2

    lax.fori_loop(0, levels, drain, 1)


def local(edge_factor, mass, rhs):
    blocks = lax.axis_size("tm")
    tiles = lax.axis_size("row")
    levels = (blocks - 1).bit_length()
    quarter, nodes = edge_factor.shape[1:]
    f32 = jnp.float32
    vmem = pl.BlockSpec(memory_space=pltpu.VMEM)
    dma = pltpu.SemaphoreType.DMA
    column = (nodes, quarter)
    mass_rows = jnp.broadcast_to(mass, (1, quarter))
    result = pl.pallas_call(
        functools.partial(kernel, blocks, levels),
        out_shape=jax.ShapeDtypeStruct(column, f32),
        in_specs=[vmem] * 3,
        out_specs=vmem,
        scratch_shapes=[
            pltpu.VMEM((tiles,) + column, f32),
            pltpu.VMEM((tiles,) + column, f32),
            pltpu.VMEM((2 * tiles + 1,) + column, f32),
            pltpu.VMEM(column, f32),
            pltpu.VMEM((tiles, quarter, nodes), f32),
            pltpu.VMEM((tiles, quarter, nodes), f32),
            pltpu.VMEM((tiles, 1, quarter), f32),
            pltpu.VMEM((levels + 1, tiles) + column, f32),
            pltpu.VMEM((levels + 1, tiles) + column, f32),
            pltpu.VMEM((levels + 1, tiles) + column, f32),
            pltpu.VMEM((levels, 2) + column, f32),
            pltpu.VMEM((levels, 2) + column, f32),
            pltpu.VMEM((levels, 4) + column, f32),
            pltpu.VMEM((levels, 2, 2) + column, f32),
            dma((4,)), dma((4,)), dma((4,)), dma((4,)), dma((3,)), dma((3,)),
            dma((levels, 32)), dma((levels, 32)),
        ],
        compiler_params=pltpu.CompilerParams(
            collective_id=0, has_side_effects=True, vmem_limit_bytes=63 * 1024 * 1024
        ),
    )(edge_factor[0], mass_rows, rhs[0])
    return result[None]


def solution(mesh):
    placed = (P("tm", "row", None), P("tm", "row"), P("tm", None, "row"))
    return jax.shard_map(
        local, mesh=mesh, in_specs=placed, out_specs=P("tm", None, "row"), check_vma=False
    )
```

time: 298 us -> 235 us (0.79)
  Pallas kernels: 294 us -> 233 us
    pallas_call x1, Pallas kernels: 294 us -> 233 us  [local(): pl.pallas_call(functools.partial(kernel, blocks, levels), out_shape=jax.S...]
where the time goes in v2:
time: 235 us
  Pallas kernels  233 us (99%)
    pallas_call x1, Pallas kernels, local(): pl.pallas_call(functools.partial(kernel, blocks, levels), out_shape=jax.S...  233 us

profile of v2, /device:TPU:16, one launch (start us, length us, event | category | flops | bytes accessed | tf_op | source)
XLA Modules:
  0.0 234.6 jit_solution(15770157089839115269)
XLA Ops:
  0.0 232.9 %shard_map.37 = f32[512,128]{1,0:T(8,128)} custom-call(f32[128,512]{1,0:T(8,128)} %bitcast.4, f32[1,128]{1,0:T(1,128)} %mass_ref.1, f32[512,128]{1,0:T(8,128)} %bitcast.5), custom_call_target="tpu_custom_call" | custom-call | tf_op jit(solution)/shard_map/pallas_call | solution.py:499
  232.9 1.7 copy.5

commit v3 on v2

--- a/solution.py
+++ b/solution.py
@@ -10,7 +10,7 @@
 MESH = pl.DeviceIdType.MESH
 EXACT = lax.Precision.HIGHEST
 Q = 128
-SPREAD = (0, 1)
+SPREAD = (1, 2)
 G = 8
 
 
@@ -166,16 +166,20 @@
         expected = expected + up.astype(jnp.int32) + down.astype(jnp.int32)
     pl.semaphore_wait(barrier, expected)
 
-    def f_copy(d):
-        return copy(f_ref, fown.at[r], fsend.at[d - 1], frecv.at[d - 1], peer(d))
-
-    def f_arrived(d):
-        return copy(f_ref, fown.at[source(d)], fsend.at[d - 1], frecv.at[d - 1], peer(d))
+    def half(h):
+        return pl.ds(h * (Q // 2), Q // 2)
+
+    def f_copy(d, h):
+        sem = d - 1 + h
+        return copy(f_ref.at[half(h)], fown.at[r, half(h)], fsend.at[sem], frecv.at[sem], peer(d))
+
+    def f_arrived(d, h):
+        sem = d - 1 + h
+        return copy(f_ref.at[half(h)], fown.at[source(d), half(h)], fsend.at[sem], frecv.at[sem], peer(d))
 
     def f_on(d, slot):
-        half = pl.ds(0 if d == 1 else Q // 2, Q // 2)
-        sem = 1 if d == 1 else 3
-        return copy(fown.at[slot, half], fown.at[slot, half], fsend.at[sem], frecv.at[sem], peer(d))
+        h = 0 if d == 1 else 1
+        return copy(fown.at[slot, half(h)], fown.at[slot, half(h)], fsend.at[4 + h], frecv.at[4 + h], peer(d))
 
     def m_copy(d):
         return copy(mass_ref, massg.at[r], msend.at[d - 1], mrecv.at[d - 1], peer(d))
@@ -188,8 +192,8 @@
         return copy(src, fnext.at[source(d)], nsend.at[d], nrecv.at[d], (t - 1, r))
 
     order = (1, 3, 2)
-    for d in (1, 3):
-        f_copy(d).start()
+    for d, h in ((1, 0), (3, 1), (1, 1), (3, 0)):
+        f_copy(d, h).start()
     for d in order:
         m_copy(d).start()
 
@@ -200,9 +204,11 @@
     fown[r] = f_ref[...]
     massg[r] = mass_ref[...]
     rcur[...] = rhs_ref[...]
-    for d in (1, 3):
-        f_arrived(d).wait_recv()
+    for d, h in ((1, 0), (3, 1)):
+        f_arrived(d, h).wait_recv()
         f_on(d, source(d)).start()
+    for d, h in ((1, 1), (3, 0)):
+        f_arrived(d, h).wait_recv()
 
         @pl.when(t >= 1)
         def _():
@@ -253,7 +259,8 @@
         lax.fori_loop(0, tiles // 2, next_gram, 0)
 
     for d in (1, 3):
-        f_copy(d).wait_send()
+        for h in range(2):
+            f_copy(d, h).wait_send()
         f_on(d, source(d)).wait_send()
     for d in order:
         m_copy(d).wait_send()
@@ -296,20 +303,23 @@
 
     def take_rows(i, s, c):
         rows = slice(c * Q, (c + 1) * Q)
-        dg[i + 1, r, rows] = dg[i, r, rows]
-
-        @pl.when(t >= s)
-        def _():
-            along(i, s, 0, c).wait_recv()
-            dg[i + 1, r, rows] = dg[i + 1, r, rows] - dr[i, 0, rows]
-
-        @pl.when(t + s < blocks)
-        def _():
-            along(i, s, 1, c).wait_recv()
-            dg[i + 1, r, rows] = dg[i + 1, r, rows] - dr[i, 1, rows]
-
-        for d in order:
-            rows_across(i, c, d, r).start()
+
+        @pl.when(r >= c)
+        def _():
+            dg[i + 1, r, rows] = dg[i, r, rows]
+
+            @pl.when(t >= s)
+            def _():
+                along(i, s, 0, c).wait_recv()
+                dg[i + 1, r, rows] = dg[i + 1, r, rows] - dr[i, 0, rows]
+
+            @pl.when(t + s < blocks)
+            def _():
+                along(i, s, 1, c).wait_recv()
+                dg[i + 1, r, rows] = dg[i + 1, r, rows] - dr[i, 1, rows]
+
+            for d in order:
+                rows_across(i, c, d, r).start()
 
     def spread_couplings(i, s, k):
         @pl.when(couples(i, s, k))
@@ -364,7 +374,7 @@
                 for d in order:
                     for c in range(tiles):
 
-                        @pl.when(j == c)
+                        @pl.when((j == c) & (source(d) >= c))
                         def _():
                             rows_across(past, c, d, source(d)).wait_recv()
 
@@ -401,6 +411,23 @@
         @pl.when(i > 0)
         def _():
             couplings_arrived(past, reach, 0)
+
+        @pl.when(down)
+        def _():
+            whiten(lg, i, 0, 1)
+            earlier = side([w[c] for c in range(tiles)])
+            terms = dot(earlier, side([w[r], w[2 * tiles]]), 0, 0)
+            staged[i, 1] = terms[:, :Q]
+            staged[i, 3] = terms[:, Q:]
+            for c in range(tiles):
+
+                @pl.when(r >= c)
+                def _():
+                    along(i, s, 1, c).start()
+
+
+        @pl.when(i > 0)
+        def _():
             couplings_arrived(past, reach, 1)
 
         @pl.when(up)
@@ -411,17 +438,11 @@
             staged[i, 0] = terms[:, :Q]
             staged[i, 2] = terms[:, Q:]
             for c in range(tiles):
-                along(i, s, 0, c).start()
-
-        @pl.when(down)
-        def _():
-            whiten(lg, i, 0, 1)
-            earlier = side([w[c] for c in range(tiles)])
-            terms = dot(earlier, side([w[r], w[2 * tiles]]), 0, 0)
-            staged[i, 1] = terms[:, :Q]
-            staged[i, 3] = terms[:, Q:]
-            for c in range(tiles):
-                along(i, s, 1, c).start()
+
+                @pl.when(r >= c)
+                def _():
+                    along(i, s, 0, c).start()
+
 
         @pl.when(up & down)
         def _():
@@ -455,15 +476,23 @@
 
         @pl.when(up)
         def _():
+            along(i, s, 4).wait_send()
             for c in range(tiles):
-                along(i, s, 0, c).wait_send()
-            along(i, s, 4).wait_send()
+
+                @pl.when(r >= c)
+                def _():
+                    along(i, s, 0, c).wait_send()
+
 
         @pl.when(down)
         def _():
+            along(i, s, 5).wait_send()
             for c in range(tiles):
-                along(i, s, 1, c).wait_send()
-            along(i, s, 5).wait_send()
+
+                @pl.when(r >= c)
+                def _():
+                    along(i, s, 1, c).wait_send()
+
 
         @pl.when(up & down)
         def _():
@@ -472,8 +501,12 @@
                 along(i, s, 3, c).wait_send()
 
         for c in range(tiles):
-            for d in order:
-                rows_across(i, c, d, r).wait_send()
+
+            @pl.when(r >= c)
+            def _():
+                for d in order:
+                    rows_across(i, c, d, r).wait_send()
+
         for k in range(2):
 
             @pl.when(couples(i, s, k))
@@ -516,7 +549,7 @@
             pltpu.VMEM((levels, 2) + column, f32),
             pltpu.VMEM((levels, 4) + column, f32),
             pltpu.VMEM((levels, 2, 2) + column, f32),
-            dma((4,)), dma((4,)), dma((4,)), dma((4,)), dma((3,)), dma((3,)),
+            dma((6,)), dma((6,)), dma((4,)), dma((4,)), dma((3,)), dma((3,)),
             dma((levels, 32)), dma((levels, 32)),
         ],
         compiler_params=pltpu.CompilerParams(

time: 235 us -> 227 us (0.966)
  Pallas kernels: 233 us -> 225 us
    pallas_call x1, Pallas kernels: 233 us -> 225 us  [local(): pl.pallas_call(functools.partial(kernel, blocks, levels), out_shape=jax.S...]
where the time goes in v3:
time: 227 us
  Pallas kernels  225 us (99%)
    pallas_call x1, Pallas kernels, local(): pl.pallas_call(functools.partial(kernel, blocks, levels), out_shape=jax.S...  225 us

profile of v3, /device:TPU:16, one launch (start us, length us, event | category | flops | bytes accessed | tf_op | source)
XLA Modules:
  0.0 227.2 jit_solution(5933998947109140737)
XLA Ops:
  0.0 225.5 %shard_map.37 = f32[512,128]{1,0:T(8,128)} custom-call(f32[128,512]{1,0:T(8,128)} %bitcast.4, f32[1,128]{1,0:T(1,128)} %mass_ref.1, f32[512,128]{1,0:T(8,128)} %bitcast.5), custom_call_target="tpu_custom_call" | custom-call | tf_op jit(solution)/shard_map/pallas_call | solution.py:532
  225.5 1.7 copy.5

commit v4 on v3

--- a/solution.py
+++ b/solution.py
@@ -404,17 +404,20 @@
 
         @pl.when(i > 0)
         def _():
+            couplings_arrived(past, reach, 0)
+
+        @pl.when(down)
+        def _():
+            whiten(lg, i, 0, 1)
+
+        @pl.when(i > 0)
+        def _():
             take_rhs(past, reach)
 
         w[2 * tiles] = under(rcur[...])
 
-        @pl.when(i > 0)
-        def _():
-            couplings_arrived(past, reach, 0)
-
         @pl.when(down)
         def _():
-            whiten(lg, i, 0, 1)
             earlier = side([w[c] for c in range(tiles)])
             terms = dot(earlier, side([w[r], w[2 * tiles]]), 0, 0)
             staged[i, 1] = terms[:, :Q]

time: 227 us -> 226 us (level)
  no operation moved by 1% of the time
where the time goes in v4:
time: 226 us
  Pallas kernels  224 us (99%)
    pallas_call x1, Pallas kernels, local(): pl.pallas_call(functools.partial(kernel, blocks, levels), out_shape=jax.S...  224 us

profile of v4, /device:TPU:16, one launch (start us, length us, event | category | flops | bytes accessed | tf_op | source)
XLA Modules:
  0.0 225.7 jit_solution(6130294569339376210)
XLA Ops:
  0.0 224.0 %shard_map.37 = f32[512,128]{1,0:T(8,128)} custom-call(f32[128,512]{1,0:T(8,128)} %bitcast.4, f32[1,128]{1,0:T(1,128)} %mass_ref.1, f32[512,128]{1,0:T(8,128)} %bitcast.5), custom_call_target="tpu_custom_call" | custom-call | tf_op jit(solution)/shard_map/pallas_call | solution.py:535
  224.0 1.7 copy.5

commit v5 on v4

--- a/solution.py
+++ b/solution.py
@@ -388,7 +388,7 @@
 
                 for k in range(2):
 
-                    @pl.when(j == SPREAD[k])
+                    @pl.when(j == SPREAD[k] - (i == 1).astype(jnp.int32))
                     def _():
                         spread_couplings(past, reach, k)
 

time: 226 us -> 225 us (level)
  no operation moved by 1% of the time
where the time goes in v5:
time: 225 us
  Pallas kernels  224 us (100%)
    pallas_call x1, Pallas kernels, local(): pl.pallas_call(functools.partial(kernel, blocks, levels), out_shape=jax.S...  224 us

profile of v5, /device:TPU:16, one launch (start us, length us, event | category | flops | bytes accessed | tf_op | source)
XLA Modules:
  0.0 225.3 jit_solution(3264281433606021256)
XLA Ops:
  0.0 223.6 %shard_map.37 = f32[512,128]{1,0:T(8,128)} custom-call(f32[128,512]{1,0:T(8,128)} %bitcast.4, f32[1,128]{1,0:T(1,128)} %mass_ref.1, f32[512,128]{1,0:T(8,128)} %bitcast.5), custom_call_target="tpu_custom_call" | custom-call | tf_op jit(solution)/shard_map/pallas_call | solution.py:535
  223.6 1.7 copy.5
